TPU v7x, 32 devices: a whole 2x2x4 slice. The times are simulated.
32 devices in a mesh: bucket: 16 (over z, y, core), edge: 2 (over x).
Axes of the slice: x: 2, y: 2, z: 4, core: 2. Of those that a mesh axis runs over, the one named last changes fastest.
Arguments:
- left_slab: bfloat16 [6144, 256], P(('bucket', 'edge')), may hold values from -1.5 to 1.5
- right_slab: bfloat16 [6144, 256], P(('bucket', 'edge')), may hold values from -1.5 to 1.5
- relation: float32 [1024, 256], replicated, may hold values from 0.5 to 1.5
- src_ids: int32 [2, 16, 4096], P(None, 'bucket', 'edge'), may hold values from 0 to 383
- dst_ids: int32 [2, 16, 4096], P(None, 'bucket', 'edge'), may hold values from 0 to 383
- rel_ids: int32 [2, 16, 4096], P(None, 'bucket', 'edge'), may hold values from 0 to 1023
- neg_ids: int32 [2, 16, 16, 512], P(None, 'bucket', 'edge'), may hold values from 0 to 383
- edge_counts: int32 [2, 16], P(None, 'bucket'), may hold values from 1 to 4096, as said below
Outputs:
- left_out: bfloat16 [6144, 256], P(('bucket', 'edge'))
- right_out: bfloat16 [6144, 256], P(('bucket', 'edge'))
- relation_out: float32 [1024, 256], replicated
Inputs may be any that keep to these rules, and one draw needn't show every extreme that they name: `edge_counts`: live edges are the first slots of a bucket; in every round some bucket has all 4096 slots live.
All inputs are finite; a program needn't handle non-finite values.
Results may differ from a plain program's by a relative error of at most 0.0046.
Values may be sent and summed in bfloat16 or wider, within the bound.
A program may use at most 64 MiB of HBM per device.

v0:
```python
import jax
import jax.numpy as jnp
from jax import lax
from jax.sharding import PartitionSpec as P

ROUNDS = 2


learn_rate = 0.05
relation_rate = 0.05


def from_behind(block, axis, distance):
    devices = range(lax.axis_size(axis))
    route = [((i - distance) % len(devices), i) for i in devices]
    return lax.ppermute(block, axis, route)


def span_grads(left, right, theta, src_c, dst_c, rel_c, neg_c, mask):
    s_rows = left[src_c]
    d_rows = right[dst_c]
    negatives = right[neg_c]
    t_rows = theta[rel_c]
    s_wide = s_rows.astype(jnp.float32)
    q_rows = (s_wide * t_rows).astype(jnp.bfloat16)
    q_wide = q_rows.astype(jnp.float32)
    d_wide = d_rows.astype(jnp.float32)
    pos = jnp.sum(q_wide * d_wide, axis=-1)
    scores = jnp.dot(q_rows, negatives.T, preferred_element_type=jnp.float32)
    g_pos = -jax.nn.sigmoid(-pos) * mask
    g_neg = (jax.nn.sigmoid(scores) * mask[:, None]).astype(jnp.bfloat16)
    g_q = g_pos[:, None] * d_wide + jnp.dot(g_neg, negatives, preferred_element_type=jnp.float32)
    g_d = g_pos[:, None] * q_wide
    g_negrows = jnp.dot(g_neg.T, q_rows, preferred_element_type=jnp.float32)
    g_s = g_q * t_rows
    g_t = g_q * s_wide
    return (g_s, g_d, g_negrows, g_t)


def train(full_left, full_right, theta, src, dst, rel, neg, block_ids, count):
    width = src.shape[1]
    n_live = jnp.sum((block_ids * width < count).astype(jnp.int32))

    def step(c, carry):
        g_left, g_right, g_theta = carry
        src_c = lax.dynamic_index_in_dim(src, c, 0, keepdims=False)
        dst_c = lax.dynamic_index_in_dim(dst, c, 0, keepdims=False)
        rel_c = lax.dynamic_index_in_dim(rel, c, 0, keepdims=False)
        neg_c = lax.dynamic_index_in_dim(neg, c, 0, keepdims=False)
        first = lax.dynamic_index_in_dim(block_ids, c, 0, keepdims=False) * width
        mask = (first + jnp.arange(width) < count).astype(jnp.float32)
        g_s, g_d, g_negrows, g_t = span_grads(
            full_left, full_right, theta, src_c, dst_c, rel_c, neg_c, mask
        )
        g_left = g_left.at[src_c].add(g_s)
        g_right = g_right.at[dst_c].add(g_d).at[neg_c].add(g_negrows)
        g_theta = g_theta.at[rel_c].add(g_t)
        return (g_left, g_right, g_theta)

    rows = full_left.shape[0]
    init = (
        jnp.zeros((rows, full_left.shape[1]), jnp.float32),
        jnp.zeros((rows, full_left.shape[1]), jnp.float32),
        jnp.zeros(theta.shape, jnp.float32),
    )
    return lax.fori_loop(0, n_live, step, init)


def relation_sum(g_theta):
    return lax.psum(g_theta, ("bucket", "edge"))


def descend(slab, grad):
    return (slab.astype(jnp.float32) - learn_rate * grad).astype(jnp.bfloat16)


def body(left_slab, right_slab, relation, src_ids, dst_ids, rel_ids, neg_ids, edge_counts):
    me = lax.axis_index("edge")
    blocks = neg_ids.shape[2]
    width = src_ids.shape[2] // blocks
    negs = neg_ids.shape[3]
    src = src_ids.reshape(ROUNDS, blocks, width)
    dst = dst_ids.reshape(ROUNDS, blocks, width)
    rel = rel_ids.reshape(ROUNDS, blocks, width)
    neg = neg_ids.reshape(ROUNDS, blocks, negs)
    positions = jnp.arange(blocks, dtype=jnp.int32)
    block_ids = me * blocks + positions
    theta = relation
    left_out = left_slab
    right_out = right_slab
    for rnd in range(ROUNDS):
        if rnd > 0:
            right_out = from_behind(right_out, "bucket", 1)
        full_left, full_right = (
            lax.all_gather(left_out, "edge", axis=0, tiled=True),
            lax.all_gather(right_out, "edge", axis=0, tiled=True),
        )
        g_left, g_right, g_theta = train(
            full_left,
            full_right,
            theta,
            src[rnd],
            dst[rnd],
            rel[rnd],
            neg[rnd],
            block_ids,
            edge_counts[rnd, 0],
        )
        g_left, g_right = (
            lax.psum_scatter(g_left, "edge", scatter_dimension=0, tiled=True),
            lax.psum_scatter(g_right, "edge", scatter_dimension=0, tiled=True),
        )
        left_out = descend(left_out, g_left)
        right_out = descend(right_out, g_right)
        theta = theta - relation_rate * relation_sum(g_theta)
    return (left_out, right_out, theta)


def solution(mesh):
    placed = (
        P(("bucket", "edge"), None),
        P(("bucket", "edge"), None),
        P(),
        P(None, "bucket", "edge"),
        P(None, "bucket", "edge"),
        P(None, "bucket", "edge"),
        P(None, "bucket", "edge", None),
        P(None, "bucket"),
    )
    return jax.shard_map(
        body,
        mesh=mesh,
        in_specs=placed,
        out_specs=(P(("bucket", "edge"), None), P(("bucket", "edge"), None), P()),
        check_vma=False,
    )
```

profile of v0, /device:TPU:0, one launch (start us, length us, event | category | flops | bytes accessed | tf_op | source)
XLA Modules:
  0.0 699.1 jit_solution(16866233475655808648)
XLA Ops:
  12.7 6.5 all_gather.12
  19.3 5.4 all_gather.13
  27.8 193.8 %while.28 = (s32[]{:T(128)}, f32[384,256]{1,0:T(8,128)}, f32[384,256]{1,0:T(8,128)S(1)}, f32[1024,256]{1,0:T(8,128)}, s32[]{:T(128)}, /*index=5*/s32[8,256]{1,0:...) while((s32[]{:T(128)}, f32[384,256]{1,0:T(8,128)}, ...), condition=%wide.region_7.8_spmd, body=%wide.region_1.7_spmd.sunk | while | flops 203302656 | bytes 9221379 | solution.py:66
  38.4 3.6 scatter_custom_fusion.31
  42.3 2.2 scatter_custom_fusion.32
  44.5 3.5 scatter_fusion
  48.0 4.0 scatter_custom_fusion.34
  62.6 3.6 scatter_custom_fusion.31
  66.4 2.2 scatter_custom_fusion.32
  68.6 3.5 scatter_fusion
  72.1 4.0 scatter_custom_fusion.34
  86.7 3.6 scatter_custom_fusion.31
  90.5 2.2 scatter_custom_fusion.32
  92.8 3.5 scatter_fusion
  96.3 4.0 scatter_custom_fusion.34
  110.9 3.6 scatter_custom_fusion.31
  114.7 2.2 scatter_custom_fusion.32
  116.9 3.5 scatter_fusion
  120.4 4.0 scatter_custom_fusion.34
  135.0 3.6 scatter_custom_fusion.31
  138.8 2.2 scatter_custom_fusion.32
  141.1 3.5 scatter_fusion
  144.6 4.0 scatter_custom_fusion.34
  159.1 3.6 scatter_custom_fusion.31
  163.0 2.2 scatter_custom_fusion.32
  165.2 3.5 scatter_fusion
  168.7 4.0 scatter_custom_fusion.34
  183.3 3.6 scatter_custom_fusion.31
  187.1 2.2 scatter_custom_fusion.32
  189.3 3.5 scatter_fusion
  192.8 4.0 scatter_custom_fusion.34
  207.4 3.6 scatter_custom_fusion.31
  211.2 2.2 scatter_custom_fusion.32
  213.5 3.5 scatter_fusion
  217.0 4.0 scatter_custom_fusion.34
  225.0 130.5 %all-reduce.3.cloned.1.call-done = f32[1024,256]{1,0:T(8,128)} async-done(((f32[1024,256]{1,0:T(8,128)}), f32[1024,256]{1,0:T(8,128)}) %all-reduce.3.cloned.1.call-update) | async-done | bytes 1048592 | tf_op jit(solution)/shard_map/psum | solution.py:70
  358.9 5.8 all_gather.14
  364.7 5.7 all_gather.15
  372.3 137.7 %while.29 = (s32[]{:T(128)}, f32[384,256]{1,0:T(8,128)}, f32[384,256]{1,0:T(8,128)S(1)}, f32[1024,256]{1,0:T(8,128)}, s32[]{:T(128)}, /*index=5*/s32[8,256]{1,0:...) while((s32[]{:T(128)}, f32[384,256]{1,0:T(8,128)}, ...), condition=%wide.region_18.19_spmd, body=%wide.region_12.18_spmd.sunk | while | flops 203302656 | bytes 9221379 | solution.py:66
  381.7 3.6 scatter_custom_fusion.38
  385.6 2.2 scatter_custom_fusion.39
  387.8 3.5 scatter_fusion.1
  391.3 4.0 scatter_custom_fusion.41
  404.6 3.6 scatter_custom_fusion.38
  408.4 2.2 scatter_custom_fusion.39
  410.6 3.5 scatter_fusion.1
  414.1 4.0 scatter_custom_fusion.41
  427.4 3.6 scatter_custom_fusion.38
  431.2 2.2 scatter_custom_fusion.39
  433.4 3.5 scatter_fusion.1
  436.9 4.0 scatter_custom_fusion.41
  450.2 3.6 scatter_custom_fusion.38
  454.0 2.2 scatter_custom_fusion.39
  456.3 3.5 scatter_fusion.1
  459.8 4.0 scatter_custom_fusion.41
  473.0 3.6 scatter_custom_fusion.38
  476.8 2.2 scatter_custom_fusion.39
  479.1 3.5 scatter_fusion.1
  482.6 4.0 scatter_custom_fusion.41
  495.8 3.6 scatter_custom_fusion.38
  501.9 3.5 scatter_fusion.1
  505.4 4.0 scatter_custom_fusion.41
  512.1 173.9 %all-reduce.5.cloned.1.call-done = f32[1024,256]{1,0:T(8,128)} async-done(((f32[1024,256]{1,0:T(8,128)}), f32[1024,256]{1,0:T(8,128)}) %all-reduce.5.cloned.1.call-update) | async-done | bytes 1048592 | tf_op jit(solution)/shard_map/psum | solution.py:70
  686.0 2.3 multiply_subtract_fusion
  (314 shorter events, 148.7 us)
Async XLA Ops:
  8.0 347.5 %all-reduce.3.cloned.1.call-start = ((), (), s32[]{:S(2)}) async-start(), calls=%async_computation.5 | async-start | bytes 2097152 | tf_op jit(solution)/shard_map/psum | solution.py:70
  8.0 0.7 copy-start.9
  9.4 1.4 copy-start.8
  9.4 3.4 copy-start.7
  10.1 2.6 copy-start.4
  12.7 6.6 copy-start.3
  19.3 8.6 %copy-start.2 = (f32[1024,256]{1,0:T(8,128)S(1)}, f32[1024,256]{1,0:T(8,128)}, u32[]{:S(2)}) copy-start(f32[1024,256]{1,0:T(8,128)} %param.14) | copy-start | bytes 3145732
  221.7 0.7 copy-start.1
  222.4 134.5 %reduce-scatter.7.cloned.1.call-start = ((), (), s32[]{:S(2)}) async-start(), calls=%async_computation.6 | async-start | bytes 589824 | tf_op jit(solution)/shard_map/reduce_scatter | solution.py:111
  223.0 135.0 %reduce-scatter.5.cloned.1.call-start = ((), (), s32[]{:S(2)}) async-start(), calls=%async_computation.4 | async-start | bytes 589824 | tf_op jit(solution)/shard_map/reduce_scatter | solution.py:110
  223.6 462.4 %all-reduce.5.cloned.1.call-start = ((), (), s32[]{:S(2)}) async-start(), calls=%async_computation.9 | async-start | bytes 2097152 | tf_op jit(solution)/shard_map/psum | solution.py:70
  357.8 6.9 collective-permute-start
  364.7 5.7 copy-start.5
  510.0 0.7 copy-start
  510.8 177.5 %reduce-scatter.9.cloned.1.call-start = ((), (), s32[]{:S(2)}) async-start(), calls=%async_computation.7 | async-start | bytes 589824 | tf_op jit(solution)/shard_map/reduce_scatter | solution.py:110
  511.3 178.6 %reduce-scatter.11.cloned.1.call-start = ((), (), s32[]{:S(2)}) async-start(), calls=%async_computation.8 | async-start | bytes 589824 | tf_op jit(solution)/shard_map/reduce_scatter | solution.py:111
  688.3 1.6 copy-start.6
Sparse Core Ops, SparseCore 0:
  221.8 133.6 all-reduce.2
  510.2 175.7 all-reduce.4
Sparse Core Ops, SparseCore 1:
  225.1 14.9 reduce-scatter.6
  242.1 13.3 reduce-scatter.4
  513.5 57.0 reduce-scatter.8
  572.8 13.3 reduce-scatter.10
where the time goes:
time: 702 us; the launch traced here: 699 us
  waiting for transfers between devices  307 us (44%)
  other arithmetic  229 us (33%)
  local copies, waits for them, and re-layouts  91.6 us (13%)
  blocking collectives  23.5 us (3%)
  loops' own time  21 us (3%)
  between operations  15.8 us (2%)
  matrix products  11.7 us (2%)
    psum x2, waiting for transfers between devices, relation_sum(): return lax.psum(g_theta, ('bucket', 'edge'))  304 us
    scatter-add x28, other arithmetic, step(): g_right = g_right.at[dst_c].add(g_d).at[neg_c].add(g_negrows)  80.1 us
    scatter-add x14, other arithmetic, step(): g_theta = g_theta.at[rel_c].add(g_t)  55.8 us
    scatter-add x14, other arithmetic, step(): g_left = g_left.at[src_c].add(g_s)  49.8 us
    gather x14, local copies, waits for them, and re-layouts, span_grads(): negatives = right[neg_c]  27.3 us
    another operation x2, loops' own time, train(): return lax.fori_loop(0, n_live, step, init)  21 us
    gather x14, local copies, waits for them, and re-layouts, span_grads(): s_rows = left[src_c]  16.1 us
    gather x14, local copies, waits for them, and re-layouts, span_grads(): d_rows = right[dst_c]  16.1 us
  transfers between devices with their start and end apart: 7, of which 2 were waited for; matrix products, arithmetic and copies ran while one was open for 1% of the time, Pallas kernels for 0%

commit v1 on v0

v1 whole, which is shorter than its diff:
```python
import functools

import jax
import jax.numpy as jnp
from jax import lax
from jax.experimental import pallas as pl
from jax.experimental.pallas import tpu as pltpu
from jax.sharding import PartitionSpec as P

MESH = pl.DeviceIdType.MESH
F32, BF16 = jnp.float32, jnp.bfloat16
learn_rate = 0.05
relation_rate = 0.05


def nn(a, b):
    return lax.dot_general(a, b, (((1,), (0,)), ((), ())), preferred_element_type=F32)


def nt(a, b):
    return lax.dot_general(a, b, (((1,), (1,)), ((), ())), preferred_element_type=F32)


def hot(ids, rows):
    return lax.broadcasted_iota(jnp.int32, (rows, ids.shape[1]), 0) == ids


def as_bf16(mask):
    return jnp.where(mask, 1.0, 0.0).astype(BF16)


def sigmoid(x):
    return 0.5 * jnp.tanh(0.5 * x) + 0.5


def kernel(
    cfg,
    count_ref, left_ref, right_ref, theta_ref, src_ref, dst_ref, rel_ref, neg_ref,
    left_out, right_out, theta_out,
    lf, rf, gl, gr, gt, counts, turned, left_t, right_t,
    gls, grs, glr, grr, moved, gts, pair_in, pair_sum, rs_in, ag,
    sem_l, sem_r, sem_gl, sem_gr, sem_pair, sem_rs, sem_ag, sem_fw,
):
    rounds, nb, ne, blocks, span, per, owners = cfg
    rows, width = left_ref.shape
    slab = rows * ne
    rels = theta_ref.shape[0]
    chips = nb // 2 * ne
    b, e = lax.axis_index("bucket"), lax.axis_index("edge")
    core = lax.rem(b, 2)
    chip = (b // 2) * ne + e
    mate = {"bucket": b + 1 - 2 * core, "edge": e}
    ahead, behind = lax.rem(b + 1, nb), lax.rem(b + nb - 1, nb)

    def chip_at(d):
        c = lax.rem(chip + d, chips)
        return c, {"bucket": 2 * (c // ne) + core, "edge": lax.rem(c, ne)}

    def edge_at(d):
        return lax.rem(e + d, ne)

    started = []

    def send(src, dst, sems, to):
        copy = pltpu.make_async_remote_copy(
            src_ref=src, dst_ref=dst, send_sem=sems.at[0], recv_sem=sems.at[1],
            device_id=to, device_id_type=MESH,
        )
        copy.start()
        started.append(copy)
        return copy

    barrier = pltpu.get_barrier_semaphore()
    for d in range(1, chips):
        pl.semaphore_signal(barrier, inc=1, device_id=chip_at(d)[1], device_id_type=MESH)
    for d in range(ne):
        for other in (ahead, behind):
            pl.semaphore_signal(
                barrier, inc=1, device_id={"bucket": other, "edge": edge_at(d)}, device_id_type=MESH
            )
    eye = as_bf16(
        lax.broadcasted_iota(jnp.int32, (width, width), 0) == lax.broadcasted_iota(jnp.int32, (width, width), 1)
    )
    lf[0, e] = left_ref[...]
    rf[0, e] = right_ref[...]
    pl.semaphore_wait(barrier, chips - 1 + 2 * ne)

    arrive = []
    for d in range(1, ne):
        to = {"bucket": b, "edge": edge_at(d)}
        arrive.append(send(left_ref, lf.at[0, e], sem_l.at[0, d], to))
        arrive.append(send(right_ref, rf.at[0, e], sem_r.at[0, d], to))

    def turn(theta):
        high = theta.astype(BF16)
        low = (theta - high.astype(F32)).astype(BF16)
        turned[pl.ds(0, width), :] = nt(eye, high).astype(BF16)
        turned[pl.ds(width, width), :] = nt(eye, low).astype(BF16)

    def count_round(r):
        ones = jnp.ones((neg_ref.shape[3], 128), BF16)

        def one(i, carry):
            ids = neg_ref[r, 0, pl.ds(i, 1), :]
            counts[r, i] = nn(as_bf16(hot(ids, slab)), ones)
            return carry

        lax.fori_loop(0, blocks, one, 0)

    turn(theta_ref[...])
    for r in range(rounds):
        count_round(r)

    edges = span * per

    for r in range(rounds):
        for copy in arrive:
            copy.wait_recv()
        arrive = []
        gl[...] = jnp.zeros_like(gl)
        gr[...] = jnp.zeros_like(gr)
        gt[...] = jnp.zeros_like(gt)
        left_t[...] = nt(eye, lf[r].reshape(slab, width)).astype(BF16)
        right_t[...] = nt(eye, rf[r].reshape(slab, width)).astype(BF16)
        live_to = count_ref[r, 0]

        def chunk(i, carry):
            at = pl.ds(pl.multiple_of(i * edges, edges), edges)
            src, dst, rel = src_ref[r, :, at], dst_ref[r, :, at], rel_ref[r, :, at]
            slot = (e * blocks + i * per) * span + lax.broadcasted_iota(jnp.int32, (1, edges), 1)
            live = jnp.where(slot < live_to, 1.0, 0.0)
            at_src = as_bf16(hot(src, slab))
            at_dst = hot(dst, slab)
            at_rel = as_bf16(hot(rel, rels))
            both = nn(turned[...], at_rel)
            t = both[:width] + both[width:]
            s = nn(left_t[...], at_src)
            q = (s * t).astype(BF16)
            scores = nn(rf[r].reshape(slab, width), q)
            pos = jnp.sum(jnp.where(at_dst, scores, 0.0), axis=0, keepdims=True)
            g_pos = -sigmoid(-pos) * live
            g_neg = (sigmoid(scores) * live).astype(BF16).astype(F32)
            many = jnp.concatenate(
                [counts[r, i * per + j] for j in range(per) for _ in range(span // 128)], axis=1
            )
            weight = (many * g_neg + jnp.where(at_dst, g_pos, 0.0)).astype(BF16)
            g_q = nn(right_t[...], weight)
            gr[...] += nt(weight, q).reshape(gr.shape)
            gl[...] += nt(at_src, (g_q * t).astype(BF16)).reshape(gl.shape)
            gt[...] += nt(at_rel, (g_q * s).astype(BF16)).reshape(gt.shape)
            return carry

        lax.fori_loop(0, blocks // per, chunk, 0)

        gts[r] = gt[...].astype(BF16).reshape(gts.shape[1:])
        pair = send(gts.at[r, 1 - core], pair_in.at[r], sem_pair.at[r], mate)
        gls[r] = gl[...].astype(BF16)
        grs[r] = gr[...].astype(BF16)
        slabs = []
        for d in range(1, ne):
            to = {"bucket": b, "edge": edge_at(d)}
            slabs.append(send(gls.at[r, edge_at(d)], glr.at[r, d], sem_gl.at[r, d], to))
            slabs.append(send(grs.at[r, edge_at(d)], grr.at[r, d], sem_gr.at[r, d], to))

        pair.wait_recv()
        pair_sum[r] = (gt[core].reshape(pair_sum.shape[1:]) + pair_in[r].astype(F32)).astype(BF16)
        parts = []

        def scatter(d):
            c, to = chip_at(d)
            return send(pair_sum.at[r, c], rs_in.at[r, d], sem_rs.at[r, d], to)

        if owners == chips:
            for d in range(1, chips):
                parts.append(scatter(d))
        else:
            for d in range(1, chips):
                @pl.when(chip_at(d)[0] < owners)
                def _():
                    scatter(d)
                    started.pop().wait_send()

        for copy in slabs:
            copy.wait_recv()
        new_l = lf[r, e].astype(F32)
        new_r = rf[r, e].astype(F32)
        g_l, g_r = gl[e], gr[e]
        for d in range(1, ne):
            g_l = g_l + glr[r, d].astype(F32)
            g_r = g_r + grr[r, d].astype(F32)
        new_l = (new_l - learn_rate * g_l).astype(BF16)
        new_r = (new_r - learn_rate * g_r).astype(BF16)
        if r == rounds - 1:
            left_out[...] = new_l
            right_out[...] = new_r
        else:
            lf[r + 1, e] = new_l
            moved[r] = new_r
            for d in range(ne):
                if d > 0:
                    to = {"bucket": b, "edge": edge_at(d)}
                    arrive.append(send(lf.at[r + 1, e], lf.at[r + 1, e], sem_l.at[r + 1, d], to))
                to = {"bucket": ahead, "edge": edge_at(d)}
                arrive.append(send(moved.at[r], rf.at[r + 1, e], sem_r.at[r + 1, d], to))

        def collect(d):
            return pltpu.make_async_remote_copy(
                src_ref=pair_sum.at[r, 0], dst_ref=rs_in.at[r, d], send_sem=sem_rs.at[r, d, 0],
                recv_sem=sem_rs.at[r, d, 1], device_id=mate, device_id_type=MESH,
            )

        def gathered(d):
            return pltpu.make_async_remote_copy(
                src_ref=pair_sum.at[r, 0], dst_ref=ag.at[r, core, 0], send_sem=sem_ag.at[r, d, 0],
                recv_sem=sem_ag.at[r, d, 1], device_id=mate, device_id_type=MESH,
            )

        def total():
            g = pair_sum[r, chip].astype(F32)
            for d in range(1, chips):
                g = g + rs_in[r, d].astype(F32)
            ag[r, core, chip] = g.astype(BF16)

        if owners == chips:
            for copy in parts:
                copy.wait_recv()
            total()
            parts = [
                send(ag.at[r, core, chip], ag.at[r, core, chip], sem_ag.at[r, d], chip_at(d)[1])
                for d in range(1, chips)
            ]
            for copy in parts:
                copy.wait_recv()
        else:
            @pl.when(chip < owners)
            def _():
                for d in range(1, chips):
                    collect(d).wait_recv()
                total()
                for d in range(1, chips):
                    send(ag.at[r, core, chip], ag.at[r, core, chip], sem_ag.at[r, d], chip_at(d)[1])
                    started.pop().wait_send()
            for d in range(1, chips):
                @pl.when(lax.rem(chip + chips - d, chips) < owners)
                def _():
                    gathered(d).wait_recv()

        send(ag.at[r, core], ag.at[r, core], sem_fw.at[r], mate).wait_recv()
        before = theta_ref[...] if r == 0 else theta_out[...]
        after = before - relation_rate * ag[r].astype(F32).reshape(rels, width)
        theta_out[...] = after
        if r < rounds - 1:
            turn(after)

    for copy in started:
        copy.wait_send()


def solution(mesh):
    nb, ne = mesh.shape["bucket"], mesh.shape["edge"]
    chips = nb // 2 * ne

    def body(left_slab, right_slab, relation, src_ids, dst_ids, rel_ids, neg_ids, edge_counts):
        rounds, _, blocks, _ = neg_ids.shape
        span = src_ids.shape[2] // blocks
        rows, width = left_slab.shape
        slab, rels = rows * ne, relation.shape[0]
        half = rels // 2
        per = 2 if slab <= 512 else 1
        owners = min(chips, half // 16)
        share = half // owners
        vmem = pl.BlockSpec(memory_space=pltpu.VMEM)
        dma = pltpu.SemaphoreType.DMA
        cfg = (rounds, nb, ne, blocks, span, per, owners)
        return pl.pallas_call(
            functools.partial(kernel, cfg),
            out_shape=(
                jax.ShapeDtypeStruct((rows, width), BF16),
                jax.ShapeDtypeStruct((rows, width), BF16),
                jax.ShapeDtypeStruct((rels, width), F32),
            ),
            in_specs=[pl.BlockSpec(memory_space=pltpu.SMEM)] + [vmem] * 7,
            out_specs=(vmem, vmem, vmem),
            scratch_shapes=[
                pltpu.VMEM((rounds, ne, rows, width), BF16),
                pltpu.VMEM((rounds, ne, rows, width), BF16),
                pltpu.VMEM((ne, rows, width), F32),
                pltpu.VMEM((ne, rows, width), F32),
                pltpu.VMEM((2, half, width), F32),
                pltpu.VMEM((rounds, blocks, slab, 128), F32),
                pltpu.VMEM((2 * width, rels), BF16),
                pltpu.VMEM((width, slab), BF16),
                pltpu.VMEM((width, slab), BF16),
                pltpu.VMEM((rounds, ne, rows, width), BF16),
                pltpu.VMEM((rounds, ne, rows, width), BF16),
                pltpu.VMEM((rounds, ne, rows, width), BF16),
                pltpu.VMEM((rounds, ne, rows, width), BF16),
                pltpu.VMEM((rounds, rows, width), BF16),
                pltpu.VMEM((rounds, 2, owners, share, width), BF16),
                pltpu.VMEM((rounds, owners, share, width), BF16),
                pltpu.VMEM((rounds, owners, share, width), BF16),
                pltpu.VMEM((rounds, chips, share, width), BF16),
                pltpu.VMEM((rounds, 2, owners, share, width), BF16),
                dma((rounds, ne, 2)),
                dma((rounds, ne, 2)),
                dma((rounds, ne, 2)),
                dma((rounds, ne, 2)),
                dma((rounds, 2)),
                dma((rounds, chips, 2)),
                dma((rounds, chips, 2)),
                dma((rounds, 2)),
            ],
            compiler_params=pltpu.CompilerParams(
                collective_id=0, has_side_effects=True, vmem_limit_bytes=60 * 1024 * 1024
            ),
        )(edge_counts, left_slab, right_slab, relation, src_ids, dst_ids, rel_ids, neg_ids)

    placed = (
        P(("bucket", "edge"), None),
        P(("bucket", "edge"), None),
        P(),
        P(None, "bucket", "edge"),
        P(None, "bucket", "edge"),
        P(None, "bucket", "edge"),
        P(None, "bucket", "edge", None),
        P(None, "bucket"),
    )
    return jax.shard_map(
        body,
        mesh=mesh,
        in_specs=placed,
        out_specs=(P(("bucket", "edge"), None), P(("bucket", "edge"), None), P()),
        check_vma=False,
    )
```

time: 702 us -> 77.1 us (0.11)
  waiting for transfers between devices: 307 us -> 0 us
  other arithmetic: 229 us -> 0 us
  local copies, waits for them, and re-layouts: 91.6 us -> 5.78 us
  Pallas kernels: 0 us -> 69.6 us
  blocking collectives: 23.5 us -> 0 us
  loops' own time: 21 us -> 0 us
  between operations: 15.8 us -> 0.65 us
  matrix products: 11.7 us -> 0 us
    psum x2 -> x0, waiting for transfers between devices: 304 us -> none  [relation_sum(): return lax.psum(g_theta, ('bucket', 'edge'))]
    scatter-add x56 -> x0, other arithmetic: 186 us -> none  [the longest x28 80.1 us: step(): g_right = g_right.at[dst_c].add(g_d).at[neg_c].add(g_negrows)]
    gather x56 -> x0, local copies, waits for them, and re-layouts: 73.1 us -> none  [the longest x14 27.3 us: span_grads(): negatives = right[neg_c]]
    pallas_call x0 -> x1, Pallas kernels: none -> 69.6 us  [body(): pl.pallas_call(functools.partial(kernel, cfg), out_shape=(jax.ShapeDtypeS...]
    all_gather x4 -> x0, blocking collectives: 23.5 us -> none  [the longest x2 12.4 us: body(): lax.all_gather(left_out, 'edge', axis=0, tiled=True)]
    another operation x2 -> x0, loops' own time: 21 us -> none  [train(): return lax.fori_loop(0, n_live, step, init)]
    convert_element_type x18 -> x0, other arithmetic: 13.9 us -> none  [the longest x14 8.72 us: step(): mask = (first + jnp.arange(width) < count).astype(jnp.float32)]
    select_n x42 -> x0, other arithmetic: 11.8 us -> none  [the longest x14 5.9 us: span_grads(): d_rows = right[dst_c]]
  transfers between devices with their start and end apart: 7 -> 0, of which waited for: 2 -> 0; matrix products, arithmetic and copies ran while one was open for 1% -> 0% of each run, Pallas kernels for 0% -> 0%
where the time goes in v1:
time: 77.1 us; the launch traced here: 76 us
  Pallas kernels  69.6 us (90%)
  local copies, waits for them, and re-layouts  5.78 us (7%)
    pallas_call x1, Pallas kernels, body(): pl.pallas_call(functools.partial(kernel, cfg), out_shape=(jax.ShapeDtypeS...  69.6 us
    unnamed x6, local copies, waits for them, and re-layouts  5.78 us

profile of v1, /device:TPU:0, one launch (start us, length us, event | category | flops | bytes accessed | tf_op | source)
XLA Modules:
  0.0 76.0 jit_solution(3431141859089185089)
XLA Ops:
  0.6 1.3 %copy.11.count_ref = s32[2,1]{1,0:T(2,128)} copy(s32[2,1]{0,1:T(1,128)} %param.15) | data formatting | bytes 16 | tf_op args[7]
  1.9 69.6 %shard_map.103 = (bf16[192,256]{1,0:T(8,128)(2,1)}, bf16[192,256]{1,0:T(8,128)(2,1)}, f32[1024,256]{1,0:T(8,128)}) custom-call(s32[2,1]{1,0:T(2,128)} %copy.11.count_ref, bf16[192,256]{1,0:T(8,128)(2,1)} %left_ref.1, bf16[192,256]{1,0:T(8,128)(2,1)} %right_ref.1, f32[1024,256]{1,0:T(8,128)} %theta_ref.1, s32[2,1,2048]{2,1,0:T(1,128)} %src_ref.1, ...), custom_call_target="tpu_custom_call" | custom-call | tf_op jit(solution)/shard_map/pallas_call | solution.py:275
  71.5 0.0 copy-start
  71.5 1.6 %copy.15 = bf16[192,256]{1,0:T(8,128)(2,1)} copy(bf16[192,256]{1,0:T(8,128)(2,1)} %get-tuple-element.6) | data formatting | bytes 196608
  73.1 0.0 copy-done
  73.1 0.6 copy.16
  73.8 2.3 %copy.17 = f32[1024,256]{1,0:T(8,128)} copy(f32[1024,256]{1,0:T(8,128)} %get-tuple-element.8) | data formatting | bytes 2097152
Async XLA Ops:
  71.5 1.6 %copy-start = (bf16[192,256]{1,0:T(8,128)(2,1)S(1)}, bf16[192,256]{1,0:T(8,128)(2,1)}, u32[]{:S(2)}) copy-start(bf16[192,256]{1,0:T(8,128)(2,1)} %get-tuple-element.7) | copy-start | bytes 294916

commit v2 on v1

--- a/solution.py
+++ b/solution.py
@@ -36,15 +36,16 @@
 def kernel(
     cfg,
     count_ref, left_ref, right_ref, theta_ref, src_ref, dst_ref, rel_ref, neg_ref,
-    left_out, right_out, theta_out,
+    left_out, right_out, theta_out, step_out,
     lf, rf, gl, gr, gt, counts, turned, left_t, right_t,
     gls, grs, glr, grr, moved, gts, pair_in, pair_sum, rs_in, ag,
     sem_l, sem_r, sem_gl, sem_gr, sem_pair, sem_rs, sem_ag, sem_fw,
 ):
-    rounds, nb, ne, blocks, span, per, owners = cfg
+    rounds, nb, ne, blocks, span, per, owners, pieces = cfg
     rows, width = left_ref.shape
     slab = rows * ne
     rels = theta_ref.shape[0]
+    half = rels // 2
     chips = nb // 2 * ne
     b, e = lax.axis_index("bucket"), lax.axis_index("edge")
     core = lax.rem(b, 2)
@@ -108,8 +109,7 @@
         lax.fori_loop(0, blocks, one, 0)
 
     turn(theta_ref[...])
-    for r in range(rounds):
-        count_round(r)
+    count_round(0)
 
     edges = span * per
 
@@ -122,7 +122,7 @@
         gt[...] = jnp.zeros_like(gt)
         left_t[...] = nt(eye, lf[r].reshape(slab, width)).astype(BF16)
         right_t[...] = nt(eye, rf[r].reshape(slab, width)).astype(BF16)
-        live_to = count_ref[r, 0]
+        live_to = count_ref[0, r]
 
         def chunk(i, carry):
             at = pl.ds(pl.multiple_of(i * edges, edges), edges)
@@ -145,51 +145,92 @@
             )
             weight = (many * g_neg + jnp.where(at_dst, g_pos, 0.0)).astype(BF16)
             g_q = nn(right_t[...], weight)
+            g_s = g_q * t
+            gs = g_s.astype(BF16)
+            gs_low = (g_s - gs.astype(F32)).astype(BF16)
             gr[...] += nt(weight, q).reshape(gr.shape)
-            gl[...] += nt(at_src, (g_q * t).astype(BF16)).reshape(gl.shape)
+            gl[...] += (nt(at_src, gs) + nt(at_src, gs_low)).reshape(gl.shape)
             gt[...] += nt(at_rel, (g_q * s).astype(BF16)).reshape(gt.shape)
             return carry
 
         lax.fori_loop(0, blocks // per, chunk, 0)
 
-        gts[r] = gt[...].astype(BF16).reshape(gts.shape[1:])
-        pair = send(gts.at[r, 1 - core], pair_in.at[r], sem_pair.at[r], mate)
-        gls[r] = gl[...].astype(BF16)
-        grs[r] = gr[...].astype(BF16)
+        for h in range(2):
+            gts[r, h] = gt[h].astype(BF16).reshape(gts.shape[2:])
+        pairs = [
+            send(gts.at[r, 1 - core, p], pair_in.at[r, p], sem_pair.at[r, p], mate) for p in range(pieces)
+        ]
+        gls[r] = gl[...].astype(gls.dtype)
+        grs[r] = gr[...].astype(grs.dtype)
         slabs = []
         for d in range(1, ne):
             to = {"bucket": b, "edge": edge_at(d)}
             slabs.append(send(gls.at[r, edge_at(d)], glr.at[r, d], sem_gl.at[r, d], to))
             slabs.append(send(grs.at[r, edge_at(d)], grr.at[r, d], sem_gr.at[r, d], to))
 
-        pair.wait_recv()
-        pair_sum[r] = (gt[core].reshape(pair_sum.shape[1:]) + pair_in[r].astype(F32)).astype(BF16)
-        parts = []
-
-        def scatter(d):
+        def scatter(p, d):
             c, to = chip_at(d)
-            return send(pair_sum.at[r, c], rs_in.at[r, d], sem_rs.at[r, d], to)
-
-        if owners == chips:
+            return send(pair_sum.at[r, p, c], rs_in.at[r, p, d], sem_rs.at[r, p, d], to)
+
+        def spread(p, d):
+            block = ag.at[r, core, p, chip]
+            return send(block, block, sem_ag.at[r, p, d], chip_at(d)[1])
+
+        def total(p):
+            g = pair_sum[r, p, chip].astype(F32)
             for d in range(1, chips):
-                parts.append(scatter(d))
-        else:
+                g = g + rs_in[r, p, d].astype(F32)
+            ag[r, core, p, chip] = g.astype(BF16)
+
+        def awaited(src, dst, sems):
+            return pltpu.make_async_remote_copy(
+                src_ref=src, dst_ref=dst, send_sem=sems.at[0], recv_sem=sems.at[1],
+                device_id=mate, device_id_type=MESH,
+            )
+
+        scattered = []
+        part = half // pieces
+        for p in range(pieces):
+            pairs[p].wait_recv()
+            own = gt[core, pl.ds(p * part, part), :].reshape(pair_sum.shape[2:])
+            pair_sum[r, p] = (own + pair_in[r, p].astype(F32)).astype(BF16)
             for d in range(1, chips):
-                @pl.when(chip_at(d)[0] < owners)
+                if owners == chips:
+                    scattered.append(scatter(p, d))
+                else:
+                    @pl.when(chip_at(d)[0] < owners)
+                    def _():
+                        scatter(p, d)
+                        started.pop().wait_send()
+
+        if r < rounds - 1:
+            count_round(r + 1)
+
+        spreads = []
+        for p in range(pieces):
+            if owners == chips:
+                for copy in scattered[p * (chips - 1):(p + 1) * (chips - 1)]:
+                    copy.wait_recv()
+                total(p)
+                spreads.append([spread(p, d) for d in range(1, chips)])
+            else:
+                @pl.when(chip < owners)
                 def _():
-                    scatter(d)
-                    started.pop().wait_send()
+                    for d in range(1, chips):
+                        awaited(pair_sum.at[r, p, 0], rs_in.at[r, p, d], sem_rs.at[r, p, d]).wait_recv()
+                    total(p)
+                    for d in range(1, chips):
+                        spread(p, d)
+                        started.pop().wait_send()
 
         for copy in slabs:
             copy.wait_recv()
-        new_l = lf[r, e].astype(F32)
-        new_r = rf[r, e].astype(F32)
         g_l, g_r = gl[e], gr[e]
         for d in range(1, ne):
             g_l = g_l + glr[r, d].astype(F32)
             g_r = g_r + grr[r, d].astype(F32)
-        new_l = (new_l - learn_rate * g_l).astype(BF16)
-        new_r = (new_r - learn_rate * g_r).astype(BF16)
+        new_l = (lf[r, e].astype(F32) - learn_rate * g_l).astype(BF16)
+        new_r = (rf[r, e].astype(F32) - learn_rate * g_r).astype(BF16)
         if r == rounds - 1:
             left_out[...] = new_l
             right_out[...] = new_r
@@ -203,57 +244,35 @@
                 to = {"bucket": ahead, "edge": edge_at(d)}
                 arrive.append(send(moved.at[r], rf.at[r + 1, e], sem_r.at[r + 1, d], to))
 
-        def collect(d):
-            return pltpu.make_async_remote_copy(
-                src_ref=pair_sum.at[r, 0], dst_ref=rs_in.at[r, d], send_sem=sem_rs.at[r, d, 0],
-                recv_sem=sem_rs.at[r, d, 1], device_id=mate, device_id_type=MESH,
-            )
-
-        def gathered(d):
-            return pltpu.make_async_remote_copy(
-                src_ref=pair_sum.at[r, 0], dst_ref=ag.at[r, core, 0], send_sem=sem_ag.at[r, d, 0],
-                recv_sem=sem_ag.at[r, d, 1], device_id=mate, device_id_type=MESH,
-            )
-
-        def total():
-            g = pair_sum[r, chip].astype(F32)
-            for d in range(1, chips):
-                g = g + rs_in[r, d].astype(F32)
-            ag[r, core, chip] = g.astype(BF16)
-
-        if owners == chips:
-            for copy in parts:
-                copy.wait_recv()
-            total()
-            parts = [
-                send(ag.at[r, core, chip], ag.at[r, core, chip], sem_ag.at[r, d], chip_at(d)[1])
-                for d in range(1, chips)
-            ]
-            for copy in parts:
-                copy.wait_recv()
+        forwards = []
+        for p in range(pieces):
+            if owners == chips:
+                for copy in spreads[p]:
+                    copy.wait_recv()
+            else:
+                for d in range(1, chips):
+                    @pl.when(lax.rem(chip + chips - d, chips) < owners)
+                    def _():
+                        awaited(pair_sum.at[r, p, 0], ag.at[r, core, p, 0], sem_ag.at[r, p, d]).wait_recv()
+            forwards.append(send(ag.at[r, core, p], ag.at[r, core, p], sem_fw.at[r, p], mate))
+        for copy in forwards:
+            copy.wait_recv()
+        if r == rounds - 1:
+            step_out[...] = ag[r].reshape(rels, width)
         else:
-            @pl.when(chip < owners)
-            def _():
-                for d in range(1, chips):
-                    collect(d).wait_recv()
-                total()
-                for d in range(1, chips):
-                    send(ag.at[r, core, chip], ag.at[r, core, chip], sem_ag.at[r, d], chip_at(d)[1])
-                    started.pop().wait_send()
-            for d in range(1, chips):
-                @pl.when(lax.rem(chip + chips - d, chips) < owners)
-                def _():
-                    gathered(d).wait_recv()
-
-        send(ag.at[r, core], ag.at[r, core], sem_fw.at[r], mate).wait_recv()
-        before = theta_ref[...] if r == 0 else theta_out[...]
-        after = before - relation_rate * ag[r].astype(F32).reshape(rels, width)
-        theta_out[...] = after
-        if r < rounds - 1:
+            before = theta_ref[...] if r == 0 else theta_out[...]
+            after = before - relation_rate * ag[r].astype(F32).reshape(rels, width)
+            theta_out[...] = after
             turn(after)
 
     for copy in started:
         copy.wait_send()
+
+
+def finish(left_ref, right_ref, theta_ref, step_ref, left_out, right_out, theta_out):
+    left_out[...] = left_ref[...]
+    right_out[...] = right_ref[...]
+    theta_out[...] = theta_ref[...] - relation_rate * step_ref[...].astype(F32)
 
 
 def solution(mesh):
@@ -266,21 +285,23 @@
         rows, width = left_slab.shape
         slab, rels = rows * ne, relation.shape[0]
         half = rels // 2
-        per = 2 if slab <= 512 else 1
+        per = 4 if slab <= 512 else 1
         owners = min(chips, half // 16)
-        share = half // owners
+        pieces = max(1, min(1, half // (16 * owners)))
+        share = half // owners // pieces
         vmem = pl.BlockSpec(memory_space=pltpu.VMEM)
         dma = pltpu.SemaphoreType.DMA
-        cfg = (rounds, nb, ne, blocks, span, per, owners)
-        return pl.pallas_call(
+        cfg = (rounds, nb, ne, blocks, span, per, owners, pieces)
+        left, right, theta, step = pl.pallas_call(
             functools.partial(kernel, cfg),
             out_shape=(
                 jax.ShapeDtypeStruct((rows, width), BF16),
                 jax.ShapeDtypeStruct((rows, width), BF16),
                 jax.ShapeDtypeStruct((rels, width), F32),
+                jax.ShapeDtypeStruct((rels, width), BF16),
             ),
             in_specs=[pl.BlockSpec(memory_space=pltpu.SMEM)] + [vmem] * 7,
-            out_specs=(vmem, vmem, vmem),
+            out_specs=(vmem, vmem, vmem, vmem),
             scratch_shapes=[
                 pltpu.VMEM((rounds, ne, rows, width), BF16),
                 pltpu.VMEM((rounds, ne, rows, width), BF16),
@@ -296,24 +317,35 @@
                 pltpu.VMEM((rounds, ne, rows, width), BF16),
                 pltpu.VMEM((rounds, ne, rows, width), BF16),
                 pltpu.VMEM((rounds, rows, width), BF16),
-                pltpu.VMEM((rounds, 2, owners, share, width), BF16),
-                pltpu.VMEM((rounds, owners, share, width), BF16),
-                pltpu.VMEM((rounds, owners, share, width), BF16),
-                pltpu.VMEM((rounds, chips, share, width), BF16),
-                pltpu.VMEM((rounds, 2, owners, share, width), BF16),
+                pltpu.VMEM((rounds, 2, pieces, owners, share, width), BF16),
+                pltpu.VMEM((rounds, pieces, owners, share, width), BF16),
+                pltpu.VMEM((rounds, pieces, owners, share, width), BF16),
+                pltpu.VMEM((rounds, pieces, chips, share, width), BF16),
+                pltpu.VMEM((rounds, 2, pieces, owners, share, width), BF16),
                 dma((rounds, ne, 2)),
                 dma((rounds, ne, 2)),
                 dma((rounds, ne, 2)),
                 dma((rounds, ne, 2)),
-                dma((rounds, 2)),
-                dma((rounds, chips, 2)),
-                dma((rounds, chips, 2)),
-                dma((rounds, 2)),
+                dma((rounds, pieces, 2)),
+                dma((rounds, pieces, chips, 2)),
+                dma((rounds, pieces, chips, 2)),
+                dma((rounds, pieces, 2)),
             ],
             compiler_params=pltpu.CompilerParams(
                 collective_id=0, has_side_effects=True, vmem_limit_bytes=60 * 1024 * 1024
             ),
-        )(edge_counts, left_slab, right_slab, relation, src_ids, dst_ids, rel_ids, neg_ids)
+        )(edge_counts.T, left_slab, right_slab, relation, src_ids, dst_ids, rel_ids, neg_ids)
+        return pl.pallas_call(
+            finish,
+            out_shape=(
+                jax.ShapeDtypeStruct((rows, width), BF16),
+                jax.ShapeDtypeStruct((rows, width), BF16),
+                jax.ShapeDtypeStruct((rels, width), F32),
+            ),
+            in_specs=[vmem] * 4,
+            out_specs=(vmem, vmem, vmem),
+            compiler_params=pltpu.CompilerParams(vmem_limit_bytes=8 * 1024 * 1024),
+        )(left, right, theta, step)
 
     placed = (
         P(("bucket", "edge"), None),

time: 77.1 us -> 74.2 us (0.962)
  local copies, waits for them, and re-layouts: 5.78 us -> 4.04 us
  Pallas kernels: 69.6 us -> 68.4 us
    pallas_call x1, Pallas kernels: 69.6 us -> 67.3 us  [body(): pl.pallas_call(functools.partial(kernel, cfg), out_shape=(jax.ShapeDtypeS...]
    unnamed x6 -> x8, local copies, waits for them, and re-layouts: 5.78 us -> 4.04 us
    pallas_call x0 -> x1, Pallas kernels: none -> 1.14 us  [body(): pl.pallas_call(finish, out_shape=(jax.ShapeDtypeStruct((rows, width), BF1...]
where the time goes in v2:
time: 74.2 us; the launch traced here: 73.1 us
  Pallas kernels  68.4 us (92%)
  local copies, waits for them, and re-layouts  4.04 us (5%)
    pallas_call x1, Pallas kernels, body(): pl.pallas_call(functools.partial(kernel, cfg), out_shape=(jax.ShapeDtypeS...  67.3 us
    unnamed x8, local copies, waits for them, and re-layouts  4.04 us

profile of v2, /device:TPU:0, one launch (start us, length us, event | category | flops | bytes accessed | tf_op | source)
XLA Modules:
  0.0 73.1 jit_solution(11678462224273669115)
XLA Ops:
  0.6 67.3 %shard_map.103 = (bf16[192,256]{1,0:T(8,128)(2,1)}, bf16[192,256]{1,0:T(8,128)(2,1)}, f32[1024,256]{1,0:T(8,128)}, bf16[1024,256]{1,0:T(8,128)(2,1)}) custom-call(s32[1,2]{1,0:T(1,128)} %bitcast.1, bf16[192,256]{1,0:T(8,128)(2,1)} %left_ref.1, bf16[192,256]{1,0:T(8,128)(2,1)} %right_ref.1, f32[1024,256]{1,0:T(8,128)} %theta_ref.1, s32[2,1,2048]{2,1,0:T(1,128)} %src_ref.1, ...), custom_call_target="tpu_custom_call" | custom-call | tf_op jit(solution)/shard_map/pallas_call | solution.py:295
  67.9 0.0 copy-start
  67.9 1.2 %copy-done = f32[1024,256]{1,0:T(8,128)S(1)} copy-done((f32[1024,256]{1,0:T(8,128)S(1)}, f32[1024,256]{1,0:T(8,128)}, u32[]{:S(2)}) %copy-start) | copy-done | bytes 1048600
  69.1 0.0 copy-start.1
  69.1 1.0 %copy-done.1 = bf16[1024,256]{1,0:T(8,128)(2,1)S(1)} copy-done((bf16[1024,256]{1,0:T(8,128)(2,1)S(1)}, bf16[1024,256]{1,0:T(8,128)(2,1)}, u32[]{:S(2)}) %copy-start.1) | copy-done | bytes 524312
  70.2 0.0 copy-start.2
  70.2 0.9 %copy-done.2 = bf16[192,256]{1,0:T(8,128)(2,1)S(1)} copy-done((bf16[192,256]{1,0:T(8,128)(2,1)S(1)}, bf16[192,256]{1,0:T(8,128)(2,1)}, u32[]{:S(2)}) %copy-start.2) | copy-done | bytes 98328
  71.1 0.0 copy-start.3
  71.1 0.9 %copy-done.3 = bf16[192,256]{1,0:T(8,128)(2,1)S(1)} copy-done((bf16[192,256]{1,0:T(8,128)(2,1)S(1)}, bf16[192,256]{1,0:T(8,128)(2,1)}, u32[]{:S(2)}) %copy-start.3) | copy-done | bytes 98328
  72.0 1.1 %shard_map.104 = (bf16[192,256]{1,0:T(8,128)(2,1)}, bf16[192,256]{1,0:T(8,128)(2,1)}, f32[1024,256]{1,0:T(8,128)}) custom-call(bf16[192,256]{1,0:T(8,128)(2,1)S(1)} %copy-done.2, bf16[192,256]{1,0:T(8,128)(2,1)S(1)} %copy-done.3, f32[1024,256]{1,0:T(8,128)S(1)} %copy-done, bf16[1024,256]{1,0:T(8,128)(2,1)S(1)} %copy-done.1), custom_call_target="tpu_custom_call" | custom-call | tf_op jit(solution)/shard_map/pallas_call | solution.py:338
Async XLA Ops:
  67.9 1.2 %copy-start = (f32[1024,256]{1,0:T(8,128)S(1)}, f32[1024,256]{1,0:T(8,128)}, u32[]{:S(2)}) copy-start(f32[1024,256]{1,0:T(8,128)} %get-tuple-element.9.theta_ref) | copy-start | bytes 3145732
  69.1 1.0 %copy-start.1 = (bf16[1024,256]{1,0:T(8,128)(2,1)S(1)}, bf16[1024,256]{1,0:T(8,128)(2,1)}, u32[]{:S(2)}) copy-start(bf16[1024,256]{1,0:T(8,128)(2,1)} %get-tuple-element.10.step_ref) | copy-start | bytes 1572868
  70.2 0.9 %copy-start.2 = (bf16[192,256]{1,0:T(8,128)(2,1)S(1)}, bf16[192,256]{1,0:T(8,128)(2,1)}, u32[]{:S(2)}) copy-start(bf16[192,256]{1,0:T(8,128)(2,1)} %get-tuple-element.7.left_ref) | copy-start | bytes 294916
  71.1 0.9 %copy-start.3 = (bf16[192,256]{1,0:T(8,128)(2,1)S(1)}, bf16[192,256]{1,0:T(8,128)(2,1)}, u32[]{:S(2)}) copy-start(bf16[192,256]{1,0:T(8,128)(2,1)} %get-tuple-element.8.right_ref) | copy-start | bytes 294916
